TPU v7x, 256 devices: a whole 4x4x8 slice. The times are simulated.
256 devices in a mesh: seq: 16 (over z, y_lo), res: 16 (over y_hi, x, core).
Axes of the slice: x: 4, y: 4 (y_hi: 2, y_lo: 2; y = y_hi * 2 + y_lo), z: 8, core: 2. Of those that a mesh axis runs over, the one named last changes fastest.
Arguments:
- target_alignment_matrix: float32 [1024, 128, 256], P('seq', 'res'), may hold values from -6 to 6
- source_alignment_matrix: float32 [1024, 128, 256], P('seq', 'res'), may hold values from -6 to 6
- source_mapping_matrix: float32 [256, 32], replicated, may hold values from -0.375 to 0.375
- target_mapping_matrix: float32 [256, 32], replicated, may hold values from -0.375 to 0.375
- final_mapping_matrix: float32 [1024, 128], replicated, may hold values from -6 to 6
- edge_offset_vector: float32 [128], replicated, may hold values from -3 to 3
- edge_delta_cotangent: float32 [128, 128, 128], P('seq', 'res'), may hold values from -6 to 6
Outputs:
- edge_delta_result: float32 [128, 128, 128], P('seq', 'res')
- grad_cols: float32 [1024, 128, 256], P('seq', 'res')
- grad_rows: float32 [1024, 128, 256], P('seq', 'res')
- grad_left: float32 [256, 32], replicated
- grad_right: float32 [256, 32], replicated
- grad_proj: float32 [1024, 128], replicated
- grad_bias: float32 [128], replicated
All inputs are finite; a program needn't handle non-finite values.
Results may differ from a plain program's by a relative error of at most 0.00013.
Values sent between devices are 32-bit elements; how exact they have to be, the bound alone decides.
A program may use at most 64 MiB of HBM per device.

v0:
```python
import jax
import jax.numpy as jnp
from jax import lax
from jax.sharding import PartitionSpec as P


def standardize_features(values):
    average = jnp.mean(values, axis=-1, keepdims=True)
    centred = values - average
    inverse = lax.rsqrt(jnp.mean(centred * centred, axis=-1, keepdims=True) + 1e-05)
    return (centred * inverse, inverse)


def normalize_back(normed, inverse, upstream):
    first = jnp.mean(upstream, axis=-1, keepdims=True)
    second = jnp.mean(upstream * normed, axis=-1, keepdims=True)
    return inverse * (upstream - first - normed * second)


def body(
    target_alignment_matrix,
    source_alignment_matrix,
    source_mapping_matrix,
    target_mapping_matrix,
    final_mapping_matrix,
    edge_offset_vector,
    edge_delta_cotangent,
):
    exact_arithmetic = lax.Precision.HIGHEST
    member_tally, amino_tally, feature_tally = target_alignment_matrix.shape
    hidden = source_mapping_matrix.shape[1]
    square = hidden * hidden
    pair_width = final_mapping_matrix.shape[1]
    seqs_total = member_tally * lax.axis_size("seq")
    own_rows = edge_delta_cotangent.shape[0]
    source_scaling_divisor, source_inverted_scale = standardize_features(source_alignment_matrix)
    target_scaling_divisor, target_inverted_scale = standardize_features(target_alignment_matrix)
    left_rows = jnp.einsum(
        "uwh,hq->uwq", source_scaling_divisor, source_mapping_matrix, precision=exact_arithmetic
    )
    right_cols = jnp.einsum(
        "iwe,ed->iwd", target_scaling_divisor, target_mapping_matrix, precision=exact_arithmetic
    )
    left_full = lax.all_gather(left_rows, "res", axis=1, tiled=True)
    slab_rows = left_full.shape[1]
    partial_value = (
        jnp.einsum("ipu,ihl->phul", left_full, right_cols, precision=exact_arithmetic) / seqs_total
    )
    partial_value = partial_value.reshape(slab_rows, amino_tally, square)
    flat_grad = edge_delta_cotangent.reshape(own_rows * amino_tally, pair_width)
    reduced = lax.psum_scatter(partial_value, "seq", scatter_dimension=0, tiled=True)
    reduced_flat = reduced.reshape(own_rows * amino_tally, square)
    edge_delta_result = (
        jnp.dot(reduced_flat, final_mapping_matrix, precision=exact_arithmetic).reshape(
            own_rows, amino_tally, pair_width
        )
        + edge_offset_vector
    )
    local_grad = jnp.dot(flat_grad, final_mapping_matrix.T, precision=exact_arithmetic).reshape(
        own_rows, amino_tally, square
    )
    grad_full = lax.all_gather(local_grad, "seq", axis=0, tiled=True)
    grad_out = jnp.einsum("pa,pb->ab", reduced_flat, flat_grad, precision=exact_arithmetic)
    grad_four = grad_full.reshape(slab_rows, amino_tally, hidden, hidden)
    grad_left_part = (
        jnp.einsum("ijhk,sjk->sih", grad_four, right_cols, precision=exact_arithmetic) / seqs_total
    )
    grad_right_side = (
        jnp.einsum("ijhk,sih->sjk", grad_four, left_full, precision=exact_arithmetic) / seqs_total
    )
    grad_left_side = lax.psum_scatter(grad_left_part, "res", scatter_dimension=1, tiled=True)
    grad_wleft = jnp.einsum(
        "sic,sih->ch", source_scaling_divisor, grad_left_side, precision=exact_arithmetic
    )
    grad_wright = jnp.einsum(
        "sjc,sjh->ch", target_scaling_divisor, grad_right_side, precision=exact_arithmetic
    )
    grad_bpart = jnp.sum(flat_grad, axis=0)
    grad_left, grad_right, grad_proj, grad_bias = lax.psum(
        (grad_wleft, grad_wright, grad_out, grad_bpart), ("seq", "res")
    )
    upstream_rows = jnp.einsum(
        "sih,ch->sic", grad_left_side, source_mapping_matrix, precision=exact_arithmetic
    )
    upstream_cols = jnp.einsum(
        "sjh,ch->sjc", grad_right_side, target_mapping_matrix, precision=exact_arithmetic
    )
    grad_rows = normalize_back(source_scaling_divisor, source_inverted_scale, upstream_rows)
    grad_cols = normalize_back(target_scaling_divisor, target_inverted_scale, upstream_cols)
    return (edge_delta_result, grad_cols, grad_rows, grad_left, grad_right, grad_proj, grad_bias)


def solution(mesh):
    in_specs = (
        P("seq", "res", None),
        P("seq", "res", None),
        P(),
        P(),
        P(),
        P(),
        P("seq", "res", None),
    )
    out_specs = (
        P("seq", "res", None),
        P("seq", "res", None),
        P("seq", "res", None),
        P(),
        P(),
        P(),
        P(),
    )
    return jax.shard_map(body, mesh=mesh, in_specs=in_specs, out_specs=out_specs, check_vma=False)
```

profile of v0, /device:TPU:2, one launch (start us, length us, event | category | flops | bytes accessed | tf_op | source)
XLA Modules:
  0.0 883.1 jit_solution(16809121184989202640)
XLA Ops:
  7.2 0.0 all-gather.5.cloned.1.call-start
  7.3 1.0 copy-done
  8.2 2.1 fusion.9
  10.4 0.0 all-gather.5.cloned.1.call-update
  10.4 0.0 all-gather.3.cloned.1.call-start
  10.4 1.2 reduce_sum.83
  11.6 1.3 multiply_reduce_fusion.2
  12.9 2.4 fusion.13
  15.3 0.0 all-gather.3.cloned.1.call-update
  15.3 0.0 reduce-scatter.5.cloned.1.call-start
  15.4 1.2 reduce_sum.81
  16.6 0.2 multiply_reduce_fusion.3
  16.8 0.6 fusion.12
  17.5 0.1 copy.44
  17.6 95.0 %all-gather.5.cloned.1.call-done = f32[128,8,1024]{2,1,0:T(8,128)} async-done(((f32[8,8,1024]{2,1,0:T(8,128)}), f32[128,8,1024]{2,1,0:T(8,128)}) %all-gather.5.cloned.1.call-update) | async-done | bytes 4194320 | tf_op jit(solution)/shard_map/all_gather | solution.py:62
  112.6 5.4 copy.41
  118.0 10.2 %bitcast_multiply_fusion = f32[64,128,32]{0,1,2:T(8,128)} fusion(f32[128,8,32,32]{0,3,2,1:T(8,128)} %bitcast.65, f32[64,8,32]{0,2,1:T(8,128)S(1)} %copy.44), kind=kOutput, calls=%fused_computation.1 | convolution fusion | flops 805568512 | bytes 5308416 | tf_op jit(solution)/shard_map/ijhk,sjk->sih/dot_general | solution.py:66
  128.2 0.0 reduce-scatter.5.cloned.1.call-update
  128.3 0.2 reduce-scatter.3.cloned.1.call-start
  128.5 50.5 %all-gather.3.cloned.1.call-done = f32[64,128,32]{2,1,0:T(8,128)} async-done(((f32[64,8,32]{2,1,0:T(8,128)}), f32[64,128,32]{2,1,0:T(8,128)}) %all-gather.3.cloned.1.call-update) | async-done | bytes 1048592 | tf_op jit(solution)/shard_map/all_gather | solution.py:44
  179.0 4.4 copy.39
  183.4 8.2 convolution_multiply_fusion
  191.6 5.6 copy.40
  197.2 0.0 reduce-scatter.3.cloned.1.call-update
  197.2 0.0 all-reduce.6.cloned.1.call-start
  197.2 0.7 copy-done.3
  197.9 0.5 reduce_sum.89
  198.4 6.8 fusion.6
  205.2 0.1 copy.43
  205.4 1.4 convolution_bitcast_fusion.1
  206.8 0.6 fusion.31
  207.4 1.1 subtract_multiply_fusion.1
  208.6 52.0 %reduce-scatter.5.cloned.1.call-done = f32[64,8,32]{0,1,2:T(8,128)} async-done(((f32[64,128,32]{0,1,2:T(8,128)}), f32[64,8,32]{0,1,2:T(8,128)}) %reduce-scatter.5.cloned.1.call-update) | async-done | bytes 65552 | tf_op jit(solution)/shard_map/reduce_scatter | solution.py:71
  260.6 1.1 copy.46
  261.7 1.4 convolution_bitcast_fusion.2
  263.0 0.6 fusion.30
  263.7 0.0 all-reduce.6.cloned.1.call-update
  263.7 0.0 all-reduce.4.cloned.1.call-start
  263.8 99.2 %reduce-scatter.3.cloned.1.call-done = f32[8,8,1024]{2,1,0:T(8,128)} async-done(((f32[128,8,1024]{2,1,0:T(8,128)}), f32[8,8,1024]{2,1,0:T(8,128)}) %reduce-scatter.3.cloned.1.call-update) | async-done | bytes 262160 | tf_op jit(solution)/shard_map/reduce_scatter | solution.py:51
  363.0 2.7 convolution_bitcast_fusion
  365.8 1.1 subtract_multiply_fusion
  366.9 2.0 convolution_add_fusion
  368.9 243.2 %all-reduce.6.cloned.1.call-done = (f32[256,32]{0,1:T(8,128)}, f32[256,32]{0,1:T(8,128)}, f32[128]{0:T(128)}) async-done(((f32[256,32]{0,1:T(8,128)}, f32[256,32]{0,1:T(8,128)}, f32[128]{0:T(128)}), (f32[256,32]{0,1:T(8,128)}, f32[256,32]{0,1:T(8,128)}, f32[128]{0:T(128)})) %all-reduce.6.cloned.1.call-update) | async-done | bytes 66064 | tf_op jit(solution)/shard_map/psum | solution.py:79
  612.1 258.4 %all-reduce.4.cloned.1.call-done = f32[1024,128]{1,0:T(8,128)} async-done(((f32[1024,128]{1,0:T(8,128)}), f32[1024,128]{1,0:T(8,128)}) %all-reduce.4.cloned.1.call-update) | async-done | bytes 524304 | tf_op jit(solution)/shard_map/psum | solution.py:79
  870.5 1.4 copy.60
  871.9 1.4 copy.61
  873.3 1.9 copy.62
  875.1 1.1 copy.63
  (21 shorter events, 0.1 us)
Async XLA Ops:
  7.2 1.0 copy-start
  7.2 9.4 %copy-start.1 = (f32[64,8,256]{2,1,0:T(8,128)S(1)}, f32[64,8,256]{2,1,0:T(8,128)}, u32[]{:S(2)}) copy-start(f32[64,8,256]{2,1,0:T(8,128)} %param.7) | copy-start | bytes 1572868
  7.2 9.6 %copy-start.4 = (f32[256,32]{0,1:T(8,128)S(1)}, f32[256,32]{0,1:T(8,128)}, u32[]{:S(2)}) copy-start(f32[256,32]{0,1:T(8,128)} %param.10) | copy-start | bytes 98308
  7.2 105.4 %all-gather.5.cloned.1.call-start = ((), (), s32[]{:S(2)}) async-start(), calls=%async_computation.4 | async-start | bytes 4456448 | tf_op jit(solution)/shard_map/all_gather | solution.py:62
  10.4 168.6 %all-gather.3.cloned.1.call-start = ((), (), s32[]{:S(2)}) async-start(), calls=%async_computation.2 | async-start | bytes 4456448 | tf_op jit(solution)/shard_map/all_gather | solution.py:44
  15.3 245.3 %reduce-scatter.5.cloned.1.call-start = ((), (), s32[]{:S(2)}) async-start(), calls=%async_computation.5 | async-start | bytes 2228224 | tf_op jit(solution)/shard_map/reduce_scatter | solution.py:71
  128.3 234.7 %reduce-scatter.3.cloned.1.call-start = ((), (), s32[]{:S(2)}) async-start(), calls=%async_computation.3 | async-start | bytes 4456448 | tf_op jit(solution)/shard_map/reduce_scatter | solution.py:51
  197.2 0.8 copy-start.3
  197.2 9.6 %copy-start.5 = (f32[256,32]{0,1:T(8,128)S(1)}, f32[256,32]{0,1:T(8,128)}, u32[]{:S(2)}) copy-start(f32[256,32]{0,1:T(8,128)} %param.10) | copy-start | bytes 98308
  197.2 414.9 %all-reduce.6.cloned.1.call-start = ((), (), s32[]{:S(2)}) async-start(), calls=%async_computation.7 | async-start | bytes 132096 | tf_op jit(solution)/shard_map/psum | solution.py:79
  205.2 56.5 %copy-start.2 = (f32[64,8,256]{2,1,0:T(8,128)S(1)}, f32[64,8,256]{2,1,0:T(8,128)}, u32[]{:S(2)}) copy-start(f32[64,8,256]{2,1,0:T(8,128)} %param.8) | copy-start | bytes 1572868
  205.2 57.8 %copy-start.6 = (f32[256,32]{0,1:T(8,128)S(1)}, f32[256,32]{0,1:T(8,128)}, u32[]{:S(2)}) copy-start(f32[256,32]{0,1:T(8,128)} %param.9) | copy-start | bytes 98308
  207.4 159.5 %copy-start.7 = (f32[128]{0:T(128)S(1)}, f32[128]{0:T(128)}, u32[]{:S(2)}) copy-start(f32[128]{0:T(128)} %param.12) | copy-start | bytes 1540
  263.7 606.8 %all-reduce.4.cloned.1.call-start = ((), (), s32[]{:S(2)}) async-start(), calls=%async_computation.6 | async-start | bytes 1048576 | tf_op jit(solution)/shard_map/psum | solution.py:79
Sparse Core Ops, SparseCore 0:
  10.5 102.0 all-gather.4
  115.7 63.2 all-gather.2
  183.3 77.3 reduce-scatter.4
  263.0 99.9 reduce-scatter.2
  369.5 242.5 all-reduce.5
  618.0 252.4 all-reduce.3
where the time goes:
time: 884 us; the launch traced here: 883 us
  waiting for transfers between devices  798 us (90%)
  matrix products  39.1 us (4%)
  local copies, waits for them, and re-layouts  24.1 us (3%)
  between operations  14.3 us (2%)
    psum x2, waiting for transfers between devices, body(): lax.psum((grad_wleft, grad_wright, grad_out, grad_bpart), ('seq', 'res'))  502 us
    reduce_scatter x1, waiting for transfers between devices, body(): lax.psum_scatter(partial_value, 'seq', scatter_dimension=0, tiled=True)  99.2 us
    all_gather x1, waiting for transfers between devices, body(): grad_full = lax.all_gather(local_grad, 'seq', axis=0, tiled=True)  95 us
    reduce_scatter x1, waiting for transfers between devices, body(): lax.psum_scatter(grad_left_part, 'res', scatter_dimension=1, tiled=True)  52 us
    all_gather x1, waiting for transfers between devices, body(): left_full = lax.all_gather(left_rows, 'res', axis=1, tiled=True)  50.5 us
  transfers between devices with their start and end apart: 6, of which 6 were waited for; matrix products, arithmetic and copies ran while one was open for 7% of the time, Pallas kernels for 0%

commit v1 on v0

--- a/solution.py
+++ b/solution.py
@@ -2,6 +2,13 @@
 import jax.numpy as jnp
 from jax import lax
 from jax.sharding import PartitionSpec as P
+
+
+def gather_over(block, axis, dim):
+    size = lax.axis_size(axis)
+    parts = jnp.stack([block for _ in range(size)])
+    parts = lax.all_to_all(parts, axis, split_axis=0, concat_axis=0)
+    return jnp.concatenate(parts, axis=dim)
 
 
 def standardize_features(values):
@@ -59,7 +66,7 @@
     local_grad = jnp.dot(flat_grad, final_mapping_matrix.T, precision=exact_arithmetic).reshape(
         own_rows, amino_tally, square
     )
-    grad_full = lax.all_gather(local_grad, "seq", axis=0, tiled=True)
+    grad_full = gather_over(local_grad, "seq", 0)
     grad_out = jnp.einsum("pa,pb->ab", reduced_flat, flat_grad, precision=exact_arithmetic)
     grad_four = grad_full.reshape(slab_rows, amino_tally, hidden, hidden)
     grad_left_part = (

time: 884 us -> 874 us (0.989)
  waiting for transfers between devices: 798 us -> 690 us
  matrix products: 39.1 us -> 98.6 us
  starting transfers between devices: 0.43 us -> 25.7 us
    all_gather x1 -> x0, waiting for transfers between devices: 95 us -> none  [body(): grad_full = lax.all_gather(local_grad, 'seq', axis=0, tiled=True)]
    all_to_all x0 -> x1, waiting for transfers between devices: none -> 94.4 us  [gather_over(): parts = lax.all_to_all(parts, axis, split_axis=0, concat_axis=0)]
    reduce_scatter x1, waiting for transfers between devices: 52 us -> 0.01 us  [body(): lax.psum_scatter(grad_left_part, 'res', scatter_dimension=1, tiled=True)]
    all_gather x1, waiting for transfers between devices: 50.5 us -> 0.02 us  [body(): left_full = lax.all_gather(left_rows, 'res', axis=1, tiled=True)]
    dot_general x1, matrix products: 6.76 us -> 43.7 us  [body(): jnp.einsum('ijhk,sih->sjk', grad_four, left_full, precision=exact_arithme...]
    dot_general x1, matrix products: 10.2 us -> 34.6 us  [body(): jnp.einsum('ijhk,sjk->sih', grad_four, right_cols, precision=exact_arithm...]
    reduce_scatter x1, starting transfers between devices: 0.22 us -> 15.8 us  [body(): lax.psum_scatter(partial_value, 'seq', scatter_dimension=0, tiled=True)]
    another operation x0 -> x2, local copies, waits for them, and re-layouts: none -> 14.2 us  [the longest x1 11.7 us: body(): grad_four = grad_full.reshape(slab_rows, amino_tally, hidden, hidden)]
  transfers between devices with their start and end apart: 6 -> 6, of which waited for: 6 -> 4; matrix products, arithmetic and copies ran while one was open for 7% -> 14% of each run, Pallas kernels for 0% -> 0%
where the time goes in v1:
time: 874 us; the launch traced here: 865 us
  waiting for transfers between devices  690 us (79%)
  matrix products  98.6 us (11%)
  local copies, waits for them, and re-layouts  32.9 us (4%)
  starting transfers between devices  25.7 us (3%)
  between operations  14.4 us (2%)
    psum x2, waiting for transfers between devices, body(): lax.psum((grad_wleft, grad_wright, grad_out, grad_bpart), ('seq', 'res'))  501 us
    all_to_all x1, waiting for transfers between devices, gather_over(): parts = lax.all_to_all(parts, axis, split_axis=0, concat_axis=0)  94.4 us
    reduce_scatter x1, waiting for transfers between devices, body(): lax.psum_scatter(partial_value, 'seq', scatter_dimension=0, tiled=True)  93.9 us
    dot_general x1, matrix products, body(): jnp.einsum('ijhk,sih->sjk', grad_four, left_full, precision=exact_arithme...  43.7 us
    dot_general x1, matrix products, body(): jnp.einsum('ijhk,sjk->sih', grad_four, right_cols, precision=exact_arithm...  34.6 us
  transfers between devices with their start and end apart: 6, of which 4 were waited for; matrix products, arithmetic and copies ran while one was open for 14% of the time, Pallas kernels for 0%

profile of v1, /device:TPU:2, one launch (start us, length us, event | category | flops | bytes accessed | tf_op | source)
XLA Modules:
  0.0 864.8 jit_solution(17547039853970959588)
XLA Ops:
  7.2 1.0 copy-done
  8.2 1.4 fusion.18
  9.6 2.5 stack.3
  12.1 9.8 %all-to-all-start = ((f32[16,8,8,1024]{3,2,1,0:T(8,128)}), f32[16,8,8,1024]{3,2,1,0:T(8,128)}, u32[]{:S(2)}, u32[]{:S(2)}) async-start(f32[16,8,8,1024]{3,2,1,0:T(8,128)} %stack.3), calls=%async_computation.1 | async-start | bytes 8388608 | tf_op jit(solution)/shard_map/all_to_all | solution.py:10
  21.9 0.0 all-gather.2.cloned.1.call-start
  22.0 0.1 reduce_sum.83
  22.1 0.2 multiply_reduce_fusion.2
  22.4 1.3 fusion.22
  23.7 0.0 all-gather.2.cloned.1.call-update
  23.7 0.0 reduce-scatter.5.cloned.1.call-start
  23.8 0.1 reduce_sum.81
  24.0 0.2 multiply_reduce_fusion.3
  24.2 0.6 fusion.21
  24.9 0.1 copy.32
  25.0 94.4 %all-to-all-done = f32[16,8,8,1024]{3,2,1,0:T(8,128)} async-done(((f32[16,8,8,1024]{3,2,1,0:T(8,128)}), f32[16,8,8,1024]{3,2,1,0:T(8,128)}, u32[]{:S(2)}, u32[]{:S(2)}) %all-to-all-start) | async-done | bytes 4194336 | tf_op jit(solution)/shard_map/all_to_all | solution.py:10
  119.4 11.7 %reshape_reshape.3 = f32[128,8,32,32]{3,2,1,0:T(8,128)} reshape(f32[16,8,8,1024]{3,2,1,0:T(8,128)} %all-to-all-done) | data formatting | bytes 8388608 | tf_op jit(solution)/shard_map/reshape;reshape | solution.py:71
  131.1 34.6 %bitcast_multiply_fusion = f32[64,128,32]{0,1,2:T(8,128)} fusion(f32[128,8,32,32]{3,2,1,0:T(8,128)} %reshape_reshape.3, f32[64,8,32]{0,2,1:T(8,128)S(1)} %copy.32), kind=kOutput, calls=%fused_computation.5 | convolution fusion | flops 805568512 | bytes 5308416 | tf_op jit(solution)/shard_map/ijhk,sjk->sih/dot_general | solution.py:73
  165.6 0.0 reduce-scatter.5.cloned.1.call-update
  165.6 15.8 %reduce-scatter.3.cloned.1.call-start = ((), (), s32[]{:S(2)}) async-start(), calls=%async_computation.4 | async-start | bytes 4456448 | tf_op jit(solution)/shard_map/reduce_scatter | solution.py:58
  181.4 0.0 all-gather.2.cloned.1.call-done
  181.4 4.4 copy.27
  185.9 8.2 convolution_multiply_fusion
  194.1 5.5 copy.28
  199.6 0.0 reduce-scatter.3.cloned.1.call-update
  199.6 0.0 all-reduce.6.cloned.1.call-start
  199.6 0.7 copy-done.4
  200.3 0.5 reduce_sum.89
  200.9 43.7 %fusion.13 = f32[64,8,32]{0,2,1:T(8,128)S(1)} fusion(f32[128,8,32,32]{3,2,1,0:T(8,128)} %reshape_reshape.3, f32[64,128,32]{0,1,2:T(8,128)S(1)} %copy.27), kind=kOutput, calls=%fused_computation.10 | convolution fusion | flops 805322752 | bytes 5308416 | tf_op jit(solution)/shard_map/ijhk,sih->sjk/dot_general | solution.py:76
  244.5 0.1 copy.31
  244.7 1.4 convolution_bitcast_fusion.1
  246.1 0.6 fusion.40
  246.7 1.1 subtract_multiply_fusion.1
  247.9 1.1 copy.34
  248.9 1.4 convolution_bitcast_fusion.2
  250.3 0.6 fusion.39
  251.0 0.0 all-reduce.6.cloned.1.call-update
  251.0 0.0 all-reduce.4.cloned.1.call-start
  251.0 93.9 %reduce-scatter.3.cloned.1.call-done = f32[8,8,1024]{2,1,0:T(8,128)} async-done(((f32[128,8,1024]{2,1,0:T(8,128)}), f32[8,8,1024]{2,1,0:T(8,128)}) %reduce-scatter.3.cloned.1.call-update) | async-done | bytes 262160 | tf_op jit(solution)/shard_map/reduce_scatter | solution.py:58
  344.9 2.7 convolution_bitcast_fusion
  347.7 0.0 all-reduce.4.cloned.1.call-update
  347.7 1.1 subtract_multiply_fusion
  348.8 2.0 convolution_add_fusion
  350.8 242.9 %all-reduce.6.cloned.1.call-done = (f32[256,32]{0,1:T(8,128)}, f32[256,32]{0,1:T(8,128)}, f32[128]{0:T(128)}) async-done(((f32[256,32]{0,1:T(8,128)}, f32[256,32]{0,1:T(8,128)}, f32[128]{0:T(128)}), (f32[256,32]{0,1:T(8,128)}, f32[256,32]{0,1:T(8,128)}, f32[128]{0:T(128)})) %all-reduce.6.cloned.1.call-update) | async-done | bytes 66064 | tf_op jit(solution)/shard_map/psum | solution.py:86
  593.8 258.4 %all-reduce.4.cloned.1.call-done = f32[1024,128]{1,0:T(8,128)} async-done(((f32[1024,128]{1,0:T(8,128)}), f32[1024,128]{1,0:T(8,128)}) %all-reduce.4.cloned.1.call-update) | async-done | bytes 524304 | tf_op jit(solution)/shard_map/psum | solution.py:86
  852.2 1.4 copy.63
  853.5 1.4 copy.64
  854.9 1.9 copy.65
  856.8 1.1 copy.66
  (25 shorter events, 0.1 us)
Async XLA Ops:
  7.2 1.0 copy-start
  12.1 9.8 %copy-start.2 = (f32[64,8,256]{2,1,0:T(8,128)S(1)}, f32[64,8,256]{2,1,0:T(8,128)}, u32[]{:S(2)}) copy-start(f32[64,8,256]{2,1,0:T(8,128)} %param.8) | copy-start | bytes 1572868
  12.1 10.3 %copy-start.7 = (f32[256,32]{0,1:T(8,128)S(1)}, f32[256,32]{0,1:T(8,128)}, u32[]{:S(2)}) copy-start(f32[256,32]{0,1:T(8,128)} %param.9) | copy-start | bytes 98308
  12.1 11.7 %copy-start.1 = (f32[64,8,256]{2,1,0:T(8,128)S(1)}, f32[64,8,256]{2,1,0:T(8,128)}, u32[]{:S(2)}) copy-start(f32[64,8,256]{2,1,0:T(8,128)} %param.7) | copy-start | bytes 1572868
  12.1 12.1 %copy-start.5 = (f32[256,32]{0,1:T(8,128)S(1)}, f32[256,32]{0,1:T(8,128)}, u32[]{:S(2)}) copy-start(f32[256,32]{0,1:T(8,128)} %param.10) | copy-start | bytes 98308
  12.1 107.2 %all-to-all-start = ((f32[16,8,8,1024]{3,2,1,0:T(8,128)}), f32[16,8,8,1024]{3,2,1,0:T(8,128)}, u32[]{:S(2)}, u32[]{:S(2)}) async-start(f32[16,8,8,1024]{3,2,1,0:T(8,128)} %stack.3), calls=%async_computation.1 | async-start | bytes 8388608 | tf_op jit(solution)/shard_map/all_to_all | solution.py:10
  21.9 159.5 %all-gather.2.cloned.1.call-start = ((), (), s32[]{:S(2)}) async-start(), calls=%async_computation.3 | async-start | bytes 4456448 | tf_op jit(solution)/shard_map/all_gather | solution.py:51
  23.7 224.1 %reduce-scatter.5.cloned.1.call-start = ((), (), s32[]{:S(2)}) async-start(), calls=%async_computation.5 | async-start | bytes 2228224 | tf_op jit(solution)/shard_map/reduce_scatter | solution.py:78
  165.6 179.3 %reduce-scatter.3.cloned.1.call-start = ((), (), s32[]{:S(2)}) async-start(), calls=%async_computation.4 | async-start | bytes 4456448 | tf_op jit(solution)/shard_map/reduce_scatter | solution.py:58
  199.6 0.8 copy-start.4
  199.6 394.2 %all-reduce.6.cloned.1.call-start = ((), (), s32[]{:S(2)}) async-start(), calls=%async_computation.7 | async-start | bytes 132096 | tf_op jit(solution)/shard_map/psum | solution.py:86
  200.9 45.2 %copy-start.6 = (f32[256,32]{0,1:T(8,128)S(1)}, f32[256,32]{0,1:T(8,128)}, u32[]{:S(2)}) copy-start(f32[256,32]{0,1:T(8,128)} %param.10) | copy-start | bytes 98308
  244.5 4.4 copy-start.3
  244.5 5.8 copy-start.8
  246.7 102.1 %copy-start.9 = (f32[128]{0:T(128)S(1)}, f32[128]{0:T(128)}, u32[]{:S(2)}) copy-start(f32[128]{0:T(128)} %param.12) | copy-start | bytes 1540
  251.0 601.2 %all-reduce.4.cloned.1.call-start = ((), (), s32[]{:S(2)}) async-start(), calls=%async_computation.6 | async-start | bytes 1048576 | tf_op jit(solution)/shard_map/psum | solution.py:86
Sparse Core Ops, SparseCore 0:
  25.8 85.8 all-gather.1
  165.8 76.9 reduce-scatter.4
  245.3 99.5 reduce-scatter.2
  351.4 242.3 all-reduce.5
  599.6 252.4 all-reduce.3
